TPU v7x, 768 devices: a whole 4x8x12 slice. The times are simulated.
768 devices in a mesh: row: 2 (over core), sec: 24 (over z_lo, y), span: 16 (over x, z_hi).
Axes of the slice: x: 4, y: 8, z: 12 (z_hi: 4, z_lo: 3; z = z_hi * 3 + z_lo), core: 2. Of those that a mesh axis runs over, the one named last changes fastest.
Arguments:
- state: float32 [2, 9, 7, 4, 64, 3072], P('row', None, None, None, 'span', 'sec'), may hold values from -6 to 6
- viscosity: float32 [2, 4, 64, 3072], P('row', None, 'span', 'sec'), may hold values from 0.1 to 1
- jacobian: float32 [2, 7, 7], P('row'), may hold values from -2 to 2
- frequency: float32 [2], P('row'), may hold values from 0.5 to 2
- offsets: int32 [9], replicated, may hold values from 0 to 3071
Outputs:
- updated: float32 [2, 9, 7, 4, 64, 3072], P('row', None, None, None, 'span', 'sec')
All inputs are finite; a program needn't handle non-finite values.
Results may differ from a plain program's by a relative error of at most 0.0001.
Values sent between devices are 32-bit elements; how exact they have to be, the bound alone decides.
A program may use at most 192 MiB of HBM per device.

v0:
```python
import math

import jax
import jax.numpy as jnp
from jax import lax
from jax.sharding import PartitionSpec as P


def from_partner(block, axis, distance):
    count = lax.axis_size(axis)
    route = []
    for low in range(count):
        high = low | 1 << distance
        if high != low and high < count:
            route += [(low, high), (high, low)]
    return lax.ppermute(block, axis, route)


def extended(block, sides, width, periodic):
    for axis, dim in sides:
        count = lax.axis_size(axis)
        forward = [(i, i + 1) for i in range(count - 1)]
        if periodic:
            forward.append((count - 1, 0))
        backward = [(target, source) for source, target in forward]
        low = lax.ppermute(
            lax.slice_in_dim(block, block.shape[dim] - width, None, axis=dim), axis, forward
        )
        high = lax.ppermute(lax.slice_in_dim(block, 0, width, axis=dim), axis, backward)
        block = jnp.concatenate([low, block, high], axis=dim)
    return block


def spectral_matrix(count):
    index = jnp.arange(count)
    offset = index[:, None] - index[None, :]
    parity = jnp.where(jnp.abs(offset) % 2 == 0, 1.0, -1.0).astype(jnp.float32)
    angle = math.pi / count * offset.astype(jnp.float32)
    safe_sin = jnp.where(offset == 0, jnp.float32(1.0), jnp.sin(angle))
    return jnp.where(offset == 0, jnp.float32(0.0), 0.5 * parity / safe_sin)


def on_device(state, viscosity, jacobian, frequency, offsets):
    flow_field_values = state[0]
    coeff = viscosity[0]
    jac_row = jacobian[0]
    omega = frequency[0]
    cells = flow_field_values.shape[-1]
    sectors = lax.axis_size("sec")
    annulus_cells = cells * sectors
    row_index = lax.axis_index("row")
    sec_index = lax.axis_index("sec")
    shift = jnp.where(row_index == 0, offsets, (annulus_cells - offsets) % annulus_cells)
    strip = flow_field_values[:, :, -1]
    other = from_partner(strip, "row", 0)
    whole = lax.all_gather(other, "sec", axis=3, tiled=True)
    local_cells = jnp.arange(cells, dtype=jnp.int32)
    source_index = (sec_index * cells + local_cells[None, :] - shift[:, None]) % annulus_cells
    ghost = jax.vmap(lambda block, where: jnp.take(block, where, axis=2))(whole, source_index)
    periodic_wrapped_state = extended(flow_field_values, (("sec", 4),), 1, True)
    plus_theta = periodic_wrapped_state[..., 2:]
    minus_theta = periodic_wrapped_state[..., :-2]
    slab_split_state = extended(flow_field_values, (("span", 3),), 1, False)
    upper_spanwise_neighbour = slab_split_state[:, :, :, 2:]
    lower_spanwise_neighbour = slab_split_state[:, :, :, :-2]
    plus_axial = jnp.concatenate([flow_field_values[:, :, 1:], ghost[:, :, None]], axis=2)
    minus_axial = jnp.concatenate(
        [jnp.zeros_like(flow_field_values[:, :, :1]), flow_field_values[:, :, :-1]], axis=2
    )
    deriv = spectral_matrix(flow_field_values.shape[0])
    timeterm = jnp.einsum(
        "tu,ufasc->tfasc", deriv, flow_field_values, precision=lax.Precision.HIGHEST
    )
    convect = jnp.einsum(
        "fg,tgasc->tfasc", jac_row, plus_theta - minus_theta, precision=lax.Precision.HIGHEST
    )
    residual = (
        -omega * timeterm
        - 0.5 * convect
        + coeff * (plus_theta + minus_theta - 2.0 * flow_field_values)
        + coeff * (upper_spanwise_neighbour + lower_spanwise_neighbour - 2.0 * flow_field_values)
        + (plus_axial + minus_axial - 2.0 * flow_field_values)
    )
    return (flow_field_values + 0.1 * residual)[None]


def solution(mesh):
    return jax.shard_map(
        on_device,
        mesh=mesh,
        in_specs=(
            P("row", None, None, None, "span", "sec"),
            P("row", None, "span", "sec"),
            P("row", None, None),
            P("row"),
            P(),
        ),
        out_specs=P("row", None, None, None, "span", "sec"),
        check_vma=False,
    )
```

profile of v0, /device:TPU:192, one launch (start us, length us, event | category | flops | bytes accessed | tf_op | source)
XLA Modules:
  0.0 229.7 jit_solution(9894356236266352284)
XLA Ops:
  6.5 0.0 copy-start.3
  6.5 0.0 all-gather.2.cloned.1.call-start
  6.5 1.2 copy.40
  7.8 1.9 collective-permute-start.4
  9.7 1.5 collective-permute-done.4
  11.2 0.0 copy-start
  11.2 0.7 copy-done
  11.9 0.0 all-gather.2.cloned.1.call-update
  12.0 9.1 %collective-permute-start.3 = (f32[9,7,4,1,128]{4,0,3,2,1:T(8,128)S(1)}, f32[9,7,4,1,128]{4,0,3,2,1:T(8,128)}, u32[]{:S(2)}, u32[]{:S(2)}) collective-permute-start(f32[9,7,4,1,128]{4,0,3,2,1:T(8,128)S(1)} %get-tuple-element.10), channel_id=1, source_target_pairs={{0,1},{1,2},{2,3},{3,4},{4,5},{5,6},{6,7},{7,8},{8,9},{9,10},{10,1... | collective-permute-start | bytes 387080 | tf_op jit(solution)/shard_map/ppermute | solution.py:26
  21.1 1.9 collective-permute-start.2
  23.0 0.3 fusion.61
  23.3 0.0 copy-start.1
  23.3 0.8 copy.17
  24.1 8.7 %collective-permute-start = (f32[9,7,4,4,1]{0,3,4,2,1:T(4,128)S(1)}, f32[9,7,4,4,1]{0,3,4,2,1:T(4,128)S(1)}, u32[]{:S(2)}, u32[]{:S(2)}) collective-permute-start(f32[9,7,4,4,1]{0,3,4,2,1:T(4,128)S(1)} %copy.17), channel_id=1, source_target_pairs={{16,0},{32,16},{48,32},{64,48},{80,64},{96,80},{112,96},{128,112},... | collective-permute-start | bytes 12104 | tf_op jit(solution)/shard_map/ppermute | solution.py:29
  32.8 0.8 copy.19
  33.6 1.9 collective-permute-start.1
  35.6 0.0 copy-done.3
  35.6 0.1 fusion.20
  35.7 1.3 fusion.60
  36.9 0.1 compare_and_fusion
  37.7 1.3 collective-permute-done
  39.0 0.8 copy.18
  39.8 8.7 %collective-permute-done.1 = f32[9,7,4,4,1]{0,3,4,2,1:T(4,128)S(1)} collective-permute-done((f32[9,7,4,4,1]{0,3,4,2,1:T(4,128)S(1)}, f32[9,7,4,4,1]{0,3,4,2,1:T(4,128)S(1)}, u32[]{:S(2)}, u32[]{:S(2)}) %collective-permute-start.1) | collective-permute-done | bytes 4064 | tf_op jit(solution)/shard_map/ppermute | solution.py:26
  48.5 0.8 copy.20
  49.3 0.8 fusion.14
  50.1 0.0 copy-done.1
  50.1 1.8 fusion.12
  51.9 0.0 copy-start.2
  51.9 103.0 %all-gather.2.cloned.1.call-done = f32[9,7,4,3072]{3,0,2,1:T(8,128)} async-done(((f32[9,7,4,128]{3,0,2,1:T(8,128)}), f32[9,7,4,3072]{3,0,2,1:T(8,128)}) %all-gather.2.cloned.1.call-update) | async-done | bytes 3096592 | tf_op jit(solution)/shard_map/all_gather | solution.py:56
  155.0 46.1 %copy.23 = f32[9,7,4,3072]{1,2,3,0:T(4,128)} copy(f32[9,7,4,3072]{3,0,2,1:T(8,128)} %all-gather.2.cloned.1.call-done) | data formatting | bytes 6193152 | tf_op jit(solution)/shard_map/all_gather | solution.py:56
  201.1 14.3 %gather_fusion = f32[1152,7,4]{1,2,0:T(4,128)} fusion(f32[9,7,4,3072]{1,2,3,0:T(4,128)} %copy.23, s32[1152]{0:T(1024)S(1)} %fusion.20), kind=kCustom, calls=%fused_computation | custom fusion | bytes 267264 | tf_op jit(solution)/shard_map/vmap(jit(_take))/gather | solution.py:59
  215.4 2.9 %copy.28 = f32[9,128,7,4]{1,0,3,2:T(8,128)S(1)} copy(f32[9,128,7,4]{2,3,1,0:T(4,128)} %bitcast.35) | data formatting | bytes 258048 | tf_op jit(solution)/shard_map/vmap(jit(_take))/gather | solution.py:59
  218.3 0.0 collective-permute-done.3
  218.4 0.0 collective-permute-done.2
  218.4 0.0 copy-done.2
  218.4 3.5 %fusion.9 = f32[1,9,7,4,4,128]{5,1,4,3,2,0:T(8,128)S(1)} fusion(f32[9,7,4,4,128]{4,0,3,2,1:T(8,128)S(1)} %bitcast.34, f32[9,7,4,1,128]{4,0,3,2,1:T(8,128)} %collective-permute-done.3, f32[9,7,4,1,128]{4,0,3,2,1:T(8,128)} %collective-permute-done.2, f32[9,7,1,4,128]{4,0,3,2,1:T(8,128)S(1)} %bitcast_select_fusion, f32[9,7,3,4,128]{4,0,3,2,1:T(8,128)} %get-tuple-element.6, ...), kind=kOutput, calls=%fused_computation.12 | convolution fusion | flops 16774902 | bytes 2725764 | tf_op jit(solution)/shard_map/tu,ufasc->tfasc/dot_general | solution.py:71
  221.9 1.0 copy.25
  (5 shorter events, 0.1 us)
Async XLA Ops:
  6.5 29.0 %copy-start.3 = (s32[9]{0:T(128)S(1)}, s32[9]{0:T(128)}, u32[]{:S(2)}) copy-start(s32[9]{0:T(128)} %param.9) | copy-start | bytes 112
  6.5 148.4 %all-gather.2.cloned.1.call-start = ((), (), s32[]{:S(2)}) async-start(), calls=%async_computation | async-start | bytes 5734400 | tf_op jit(solution)/shard_map/all_gather | solution.py:56
  7.8 3.4 %collective-permute-start.4 = (f32[9,7,4,128]{3,0,2,1:T(8,128)S(1)}, f32[9,7,4,128]{3,0,2,1:T(8,128)S(1)}, u32[]{:S(2)}, u32[]{:S(2)}) collective-permute-start(f32[9,7,4,128]{3,0,2,1:T(8,128)S(1)} %slice_bitcast_fusion), channel_id=1, source_target_pairs={{0,384},{384,0},{1,385},{385,1},{2,386},{386,2},{3,387},{387,3},{4... | collective-permute-start | bytes 387080 | tf_op jit(solution)/shard_map/ppermute | solution.py:16
  11.2 0.7 copy-start
  12.0 206.4 %collective-permute-start.3 = (f32[9,7,4,1,128]{4,0,3,2,1:T(8,128)S(1)}, f32[9,7,4,1,128]{4,0,3,2,1:T(8,128)}, u32[]{:S(2)}, u32[]{:S(2)}) collective-permute-start(f32[9,7,4,1,128]{4,0,3,2,1:T(8,128)S(1)} %get-tuple-element.10), channel_id=1, source_target_pairs={{0,1},{1,2},{2,3},{3,4},{4,5},{5,6},{6,7},{7,8},{8,9},{9,10},{10,1... | collective-permute-start | bytes 387080 | tf_op jit(solution)/shard_map/ppermute | solution.py:26
  21.1 197.3 %collective-permute-start.2 = (f32[9,7,4,1,128]{4,0,3,2,1:T(8,128)S(1)}, f32[9,7,4,1,128]{4,0,3,2,1:T(8,128)}, u32[]{:S(2)}, u32[]{:S(2)}) collective-permute-start(f32[9,7,4,1,128]{4,0,3,2,1:T(8,128)S(1)} %get-tuple-element.9), channel_id=1, source_target_pairs={{1,0},{2,1},{3,2},{4,3},{5,4},{6,5},{7,6},{8,7},{9,8},{10,9},{11,1... | collective-permute-start | bytes 387080 | tf_op jit(solution)/shard_map/ppermute | solution.py:29
  23.3 26.8 %copy-start.1 = (f32[1,7,7]{2,0,1:T(1,128)S(1)}, f32[1,7,7]{2,0,1:T(1,128)}, u32[]{:S(2)}) copy-start(f32[1,7,7]{2,0,1:T(1,128)} %param.7) | copy-start | bytes 592
  24.1 14.9 %collective-permute-start = (f32[9,7,4,4,1]{0,3,4,2,1:T(4,128)S(1)}, f32[9,7,4,4,1]{0,3,4,2,1:T(4,128)S(1)}, u32[]{:S(2)}, u32[]{:S(2)}) collective-permute-start(f32[9,7,4,4,1]{0,3,4,2,1:T(4,128)S(1)} %copy.17), channel_id=1, source_target_pairs={{16,0},{32,16},{48,32},{64,48},{80,64},{96,80},{112,96},{128,112},... | collective-permute-start | bytes 12104 | tf_op jit(solution)/shard_map/ppermute | solution.py:29
  33.6 14.9 %collective-permute-start.1 = (f32[9,7,4,4,1]{0,3,4,2,1:T(4,128)S(1)}, f32[9,7,4,4,1]{0,3,4,2,1:T(4,128)S(1)}, u32[]{:S(2)}, u32[]{:S(2)}) collective-permute-start(f32[9,7,4,4,1]{0,3,4,2,1:T(4,128)S(1)} %copy.19), channel_id=1, source_target_pairs={{0,16},{16,32},{32,48},{48,64},{64,80},{80,96},{96,112},{112,128},... | collective-permute-start | bytes 12104 | tf_op jit(solution)/shard_map/ppermute | solution.py:26
  51.9 166.5 %copy-start.2 = (f32[1,4,4,128]{3,2,1,0:T(4,128)S(1)}, f32[1,4,4,128]{3,2,1,0:T(4,128)}, u32[]{:S(2)}) copy-start(f32[1,4,4,128]{3,2,1,0:T(4,128)} %param.6) | copy-start | bytes 24580
Sparse Core Ops, SparseCore 0:
  12.0 142.8 all-gather.1
where the time goes:
time: 231 us; the launch traced here: 230 us
  waiting for transfers between devices  115 us (50%)
  local copies, waits for them, and re-layouts  71.1 us (31%)
  starting transfers between devices  23.6 us (10%)
  between operations  14.2 us (6%)
  matrix products  5.26 us (2%)
    all_gather x1, waiting for transfers between devices, on_device(): whole = lax.all_gather(other, 'sec', axis=3, tiled=True)  103 us
    all_gather x1, local copies, waits for them, and re-layouts, on_device(): whole = lax.all_gather(other, 'sec', axis=3, tiled=True)  46.1 us
    gather x2, local copies, waits for them, and re-layouts, on_device(): jnp.take(block, where, axis=2)  17.2 us
    ppermute x2, starting transfers between devices, extended(): lax.ppermute(lax.slice_in_dim(block, block.shape[dim] - width, None, axis...  11 us
    ppermute x2, starting transfers between devices, extended(): lax.ppermute(lax.slice_in_dim(block, 0, width, axis=dim), axis, backward)  10.6 us
    ppermute x2, waiting for transfers between devices, extended(): lax.ppermute(lax.slice_in_dim(block, block.shape[dim] - width, None, axis...  8.71 us
  transfers between devices with their start and end apart: 6, of which 4 were waited for; matrix products, arithmetic and copies ran while one was open for 31% of the time, Pallas kernels for 0%

commit v1 on v0

v1 whole, which is shorter than its diff:
```python
import functools
import math

import jax
import jax.numpy as jnp
from jax import lax
from jax.experimental import pallas as pl
from jax.experimental.pallas import tpu as pltpu
from jax.sharding import PartitionSpec as P

MESH = pl.DeviceIdType.MESH
LANES = 128


def kernel(
    sectors, slabs, times, fields, share,
    strip_src, state_src, visc_src, jac, freq, offs, out,
    state, strip, coeff, total,
    edge_up, edge_down, from_up, from_down,
    edges, edges_left, edges_right,
    gathered, turned, ghost,
    load_sem, send_sem, recv_sem,
):
    row = lax.axis_index("row")
    me = lax.axis_index("sec")
    slab = lax.axis_index("span")
    planes = times * fields
    holders = planes // share
    cells = planes * 4
    annulus = sectors * LANES

    loads = (
        pltpu.make_async_copy(strip_src.at[:, 3], strip, load_sem.at[0]),
        pltpu.make_async_copy(state_src, state, load_sem.at[1]),
        pltpu.make_async_copy(visc_src, coeff, load_sem.at[2]),
    )
    for load in loads:
        load.start()

    right = lax.rem(me + 1, sectors)
    left = lax.rem(me + (sectors - 1), sectors)
    has_up = slab < slabs - 1
    has_down = slab > 0

    barrier = pltpu.get_barrier_semaphore()

    @pl.loop(0, sectors)
    def _(step):
        target = lax.rem(me + step, sectors)
        pl.semaphore_signal(
            barrier, inc=1, device_id={"row": 1 - row, "sec": target}, device_id_type=MESH
        )

        @pl.when(step > 0)
        def _():
            pl.semaphore_signal(
                barrier, inc=1, device_id={"sec": target}, device_id_type=MESH
            )

    @pl.when(has_up)
    def _():
        pl.semaphore_signal(barrier, inc=1, device_id={"span": slab + 1}, device_id_type=MESH)

    @pl.when(has_down)
    def _():
        pl.semaphore_signal(barrier, inc=1, device_id={"span": slab - 1}, device_id_type=MESH)

    for load in loads:
        load.wait()

    edge_up[...] = state[pl.ds(3, cells, stride=4), :]
    edge_down[...] = state[pl.ds(0, cells, stride=4), :]
    lane = lax.broadcasted_iota(jnp.int32, (8, LANES), 1)
    sub = lax.broadcasted_iota(jnp.int32, (8, LANES), 0)

    def rows_of(t, f, half):
        return pl.ds(pl.multiple_of(t * (fields * 16) + (f * 16 + half * 8), 8), 8)

    def pack(t, held):
        packed = []
        for half in range(2):
            part = jnp.zeros((8, LANES), jnp.float32)
            for f in range(fields):
                turn = pltpu.roll(state[rows_of(t, f, half), :], 2 * f + 1, 1)
                part = jnp.where((lane >> 1) == f, turn, part)
            packed.append(held[half] + pltpu.roll(part, t * (2 * fields), 1))
        return tuple(packed)

    zero = jnp.zeros((8, LANES), jnp.float32)
    packed = lax.fori_loop(0, times, pack, (zero, zero))
    edges[pl.ds(0, 8), :] = packed[0]
    edges[pl.ds(8, 8), :] = packed[1]

    pl.semaphore_wait(
        barrier, 2 * sectors - 1 + has_up.astype(jnp.int32) + has_down.astype(jnp.int32)
    )

    @pl.loop(0, sectors)
    def _(step):
        target = lax.rem(me + step, sectors)

        @pl.when(target < holders)
        def _():
            pltpu.make_async_remote_copy(
                src_ref=strip.at[pl.ds(share * target, share)],
                dst_ref=gathered.at[me],
                send_sem=send_sem.at[0],
                recv_sem=recv_sem.at[0],
                device_id={"row": 1 - row, "sec": target},
                device_id_type=MESH,
            ).start()

    to_right = pltpu.make_async_remote_copy(
        src_ref=edges, dst_ref=edges_left, send_sem=send_sem.at[1], recv_sem=recv_sem.at[1],
        device_id={"sec": right}, device_id_type=MESH,
    )
    to_left = pltpu.make_async_remote_copy(
        src_ref=edges, dst_ref=edges_right, send_sem=send_sem.at[2], recv_sem=recv_sem.at[2],
        device_id={"sec": left}, device_id_type=MESH,
    )
    to_right.start()
    to_left.start()
    to_up = pltpu.make_async_remote_copy(
        src_ref=edge_up, dst_ref=from_down, send_sem=send_sem.at[3], recv_sem=recv_sem.at[3],
        device_id={"span": slab + 1}, device_id_type=MESH,
    )
    to_down = pltpu.make_async_remote_copy(
        src_ref=edge_down, dst_ref=from_up, send_sem=send_sem.at[4], recv_sem=recv_sem.at[4],
        device_id={"span": slab - 1}, device_id_type=MESH,
    )

    @pl.when(has_up)
    def _():
        to_up.start()

    @pl.when(has_down)
    def _():
        to_down.start()

    weights = [
        freq[0] * jnp.float32(-0.05 * (-1.0) ** m / math.sin(math.pi * m / times))
        for m in range(1, times // 2 + 1)
    ]

    @pl.loop(0, fields)
    def _(f):
        for half in range(2):
            at = [
                pl.ds(pl.multiple_of(f * 16 + (t * fields * 16 + half * 8), 8), 8)
                for t in range(times)
            ]
            values = [state[at[t], :] for t in range(times)]
            for t in range(times):
                acc = None
                for m, weight in enumerate(weights, 1):
                    term = weight * (values[(t - m) % times] - values[(t + m) % times])
                    acc = term if acc is None else acc + term
                total[at[t], :] = acc

    @pl.when(me < holders)
    def _():
        pltpu.make_async_copy(gathered, gathered, recv_sem.at[0]).wait()
        thin = lax.broadcasted_iota(jnp.int32, (4, LANES), 1)
        for part in range(share):
            offset = offs[(share * me + part) // fields]
            shift = jnp.where(row == 0, offset, annulus - offset)
            whole = shift >> 7
            rest = shift & (LANES - 1)
            before = pltpu.roll(
                gathered[lax.rem(2 * sectors - 1 - whole, sectors), part], rest, 1
            )
            for sector in range(sectors):
                after = pltpu.roll(
                    gathered[lax.rem(2 * sectors + sector - whole, sectors), part], rest, 1
                )
                turned[sector, part] = jnp.where(thin >= rest, after, before)
                before = after
        pltpu.make_async_copy(
            turned.at[me], ghost.at[pl.ds(share * me, share)], recv_sem.at[5]
        ).start()

        @pl.loop(1, sectors)
        def _(step):
            target = lax.rem(me + step, sectors)
            pltpu.make_async_remote_copy(
                src_ref=turned.at[target],
                dst_ref=ghost.at[pl.ds(share * me, share)],
                send_sem=send_sem.at[5],
                recv_sem=recv_sem.at[5],
                device_id={"sec": target},
                device_id_type=MESH,
            ).start()

    to_right.wait_recv()
    to_left.wait_recv()
    mix = [[jac[f, 0, g] * jnp.float32(-0.05) for g in range(fields)] for f in range(fields)]
    diffuse = [coeff[pl.ds(8 * half, 8), :] * jnp.float32(0.1) for half in range(2)]
    first_span = (sub & 3) == 0
    last_span = (sub & 3) == 3
    low = sub < 4

    @pl.loop(0, times)
    def _(t):
        turn = lax.rem(LANES - t * (2 * fields), LANES)
        lefts = [pltpu.roll(edges_left[pl.ds(8 * h, 8), :], turn, 1) for h in range(2)]
        rights = [pltpu.roll(edges_right[pl.ds(8 * h, 8), :], turn, 1) for h in range(2)]
        slopes = []
        for f in range(fields):
            pair = [state[rows_of(t, f, half), :] for half in range(2)]
            swapped = [pltpu.roll(v, 4, 0) for v in pair]
            middle = jnp.where(low, swapped[0], swapped[1])
            axial = (
                middle + jnp.where(low, 0.0, swapped[0]),
                middle + jnp.where(low, swapped[1], 0.0),
            )
            slope = []
            for half in range(2):
                v = pair[half]
                plus = jnp.where(
                    lane == LANES - 1,
                    pltpu.roll(rights[half], (LANES - 2 - 2 * f) % LANES, 1),
                    pltpu.roll(v, LANES - 1, 1),
                )
                minus = jnp.where(
                    lane == 0,
                    pltpu.roll(lefts[half], (LANES - 2 * f) % LANES, 1),
                    pltpu.roll(v, 1, 1),
                )
                around = plus + minus
                slope.append(plus - minus)
                around = around + jnp.where(last_span, 0.0, pltpu.roll(v, 7, 0))
                around = around + jnp.where(first_span, 0.0, pltpu.roll(v, 1, 0))
                at = rows_of(t, f, half)
                total[at, :] = (
                    total[at, :]
                    + 0.8 * v
                    + 0.1 * axial[half]
                    + diffuse[half] * (around - 4.0 * v)
                )
            slopes.append(slope)
        for f in range(fields):
            for half in range(2):
                acc = mix[f][0] * slopes[0][half]
                for g in range(1, fields):
                    acc = acc + mix[f][g] * slopes[g][half]
                at = rows_of(t, f, half)
                total[at, :] = total[at, :] + acc

    def span_weights(s):
        rows = [coeff[pl.ds(4 * a + s, 1), :] * jnp.float32(0.1) for a in range(4)]
        out = jnp.broadcast_to(rows[3], (8, LANES))
        for a in range(3):
            out = jnp.where((sub & 3) == a, jnp.broadcast_to(rows[a], (8, LANES)), out)
        return out

    def add_span(source, s):
        weight = span_weights(s)
        whole = cells // 8
        for block in range(whole):
            at = pl.ds(block * 32 + s, 8, stride=4)
            total[at, :] = total[at, :] + weight * source[pl.ds(block * 8, 8), :]
        if cells % 8:
            at = pl.ds(whole * 32 + s, cells % 8, stride=4)
            total[at, :] = (
                total[at, :]
                + weight[: cells % 8] * source[pl.ds(whole * 8, cells % 8), :]
            )

    @pl.when(has_up)
    def _():
        to_down.wait_recv()
        add_span(from_up, 3)

    @pl.when(has_down)
    def _():
        to_up.wait_recv()
        add_span(from_down, 0)

    pltpu.make_async_copy(ghost, ghost, recv_sem.at[5]).wait()
    for n in range(planes):
        at = pl.ds(16 * n + 12, 4)
        total[at, :] = total[at, :] + 0.1 * ghost[n]

    store = pltpu.make_async_copy(total, out, load_sem.at[0])
    store.start()
    pltpu.make_async_copy(strip, strip, send_sem.at[0]).wait()
    to_right.wait_send()
    to_left.wait_send()

    @pl.when(has_up)
    def _():
        to_up.wait_send()

    @pl.when(has_down)
    def _():
        to_down.wait_send()

    @pl.when(me < holders)
    def _():
        others = turned.at[pl.ds(0, sectors - 1)]
        pltpu.make_async_copy(others, others, send_sem.at[5]).wait()

    store.wait()


def solution(mesh):
    sectors, slabs = mesh.shape["sec"], mesh.shape["span"]

    def on_device(state, viscosity, jacobian, frequency, offsets):
        _, times, fields, axial, span, lanes = state.shape
        planes = times * fields
        share = next(
            s for s in range(-(-planes // sectors), planes + 1) if planes % s == 0
        )
        rows = planes * axial * span
        edge = pltpu.VMEM((planes * axial, lanes), jnp.float32)
        pairs = pltpu.VMEM((16, lanes), jnp.float32)
        anywhere = pl.BlockSpec(memory_space=pl.ANY)
        scalars = pl.BlockSpec(memory_space=pltpu.SMEM)
        out = pl.pallas_call(
            functools.partial(kernel, sectors, slabs, times, fields, share),
            out_shape=jax.ShapeDtypeStruct((rows, lanes), jnp.float32),
            in_specs=[anywhere] * 3 + [scalars] * 3,
            out_specs=anywhere,
            scratch_shapes=[
                pltpu.VMEM((rows, lanes), jnp.float32),
                pltpu.VMEM((planes, span, lanes), jnp.float32),
                pltpu.VMEM((16, lanes), jnp.float32),
                pltpu.VMEM((rows, lanes), jnp.float32),
                edge, edge, edge, edge,
                pairs, pairs, pairs,
                pltpu.VMEM((sectors, share, span, lanes), jnp.float32),
                pltpu.VMEM((sectors, share, span, lanes), jnp.float32),
                pltpu.VMEM((planes, span, lanes), jnp.float32),
                pltpu.SemaphoreType.DMA((3,)),
                pltpu.SemaphoreType.DMA((6,)),
                pltpu.SemaphoreType.DMA((6,)),
            ],
            compiler_params=pltpu.CompilerParams(collective_id=0, has_side_effects=True),
        )(
            state.reshape(planes, axial, span, lanes),
            state.reshape(rows, lanes),
            viscosity.reshape(axial * span, lanes),
            jacobian.reshape(fields, 1, fields),
            frequency,
            offsets,
        )
        return out.reshape(state.shape)

    return jax.shard_map(
        on_device,
        mesh=mesh,
        in_specs=(
            P("row", None, None, None, "span", "sec"),
            P("row", None, "span", "sec"),
            P("row", None, None),
            P("row"),
            P(),
        ),
        out_specs=P("row", None, None, None, "span", "sec"),
        check_vma=False,
    )
```

time: 231 us -> 36.9 us (0.16)
  the two profiles are of different devices: /device:TPU:192 before, /device:TPU:5 now
where the time goes in v1:
time: 36.9 us; the launch traced here: 36.7 us
  Pallas kernels  34.1 us (92%)
  local copies, waits for them, and re-layouts  1.86 us (5%)
  between operations  0.66 us (2%)
    pallas_call x1, Pallas kernels, on_device(): pl.pallas_call(functools.partial(kernel, sectors, slabs, times, fields, s...  34.1 us
    unnamed x1, local copies, waits for them, and re-layouts  1.86 us

profile of v1, /device:TPU:5, one launch (start us, length us, event | category | flops | bytes accessed | tf_op | source)
XLA Modules:
  0.0 36.7 jit_solution(11555950127108719299)
XLA Ops:
  0.7 34.1 %shard_map.55 = f32[1008,128]{1,0:T(8,128)} custom-call(f32[63,4,4,128]{3,2,1,0:T(4,128)} %bitcast.5, f32[1008,128]{1,0:T(8,128)} %bitcast.6, f32[16,128]{1,0:T(8,128)} %bitcast.8, f32[7,1,7]{2,1,0:T(1,128)} %bitcast.9, f32[1]{0:T(128)S(6)} %copy.7.freq, s32[9]{0:T(128)} %offs.1), custom_call_target="tpu_custom_call" | custom-call | tf_op jit(solution)/shard_map/pallas_call | solution.py:320
  34.8 1.9 %copy.8 = f32[1,9,7,4,4,128]{5,4,3,2,1,0:T(4,128)} copy(f32[1,9,7,4,4,128]{5,4,3,2,1,0:T(4,128)} %bitcast.7) | data formatting | bytes 1032192

commit v2 on v1

--- a/solution.py
+++ b/solution.py
@@ -10,66 +10,177 @@
 
 MESH = pl.DeviceIdType.MESH
 LANES = 128
+DEPTHS = 4
+AWAY = (0, 12, 20)
 
 
 def kernel(
-    sectors, slabs, times, fields, share,
-    strip_src, state_src, visc_src, jac, freq, offs, out,
-    state, strip, coeff, total,
+    sectors, slabs, times, fields, share, away,
+    strip_src, state_src, visc_src, jac_src, freq_src, offs_src, total,
+    state, coeff, jac, freq, offs,
     edge_up, edge_down, from_up, from_down,
     edges, edges_left, edges_right,
     gathered, turned, ghost,
-    load_sem, send_sem, recv_sem,
+    load_sem, send_sem, recv_sem, ready_sem, home_sem,
 ):
     row = lax.axis_index("row")
     me = lax.axis_index("sec")
     slab = lax.axis_index("span")
     planes = times * fields
-    holders = planes // share
     cells = planes * 4
     annulus = sectors * LANES
 
+    right = lax.rem(me + 1, sectors)
+    left = lax.rem(me + (sectors - 1), sectors)
+
+    def is_holder(sector):
+        held = sector != away[0]
+        for other in away[1:]:
+            held = held & (sector != other)
+        return held
+
+    def rank(sector):
+        before = sector
+        for other in away:
+            before = before - jnp.where(sector > other, 1, 0)
+        return before
+
+    is_home = is_holder(me)
+    mine = rank(me)
+
+    depth = lax.rem(slab, DEPTHS)
+    ordered = depth == DEPTHS - 1
+    is_root = (row == 0) & (me == 0) & (slab == 0)
+
+    def lateness(at_row, sector):
+        along = sector & 7
+        late = 10 * jnp.minimum(along, 8 - along) + jnp.where(along > 3, 10, 0) + jnp.where(sector > 15, 14, 0)
+        return late * (2 * sectors) + 2 * sector + at_row
+
+    here = lateness(row, me)
+
+    def root_at(at_row, sector):
+        return (at_row == 0) & (sector == 0) & (slab == 0)
+
+    def is_later(at_row, sector):
+        return root_at(at_row, sector) | (ordered & ~is_root & (lateness(at_row, sector) > here))
+
+    targets = [lax.rem(me + step, sectors) for step in range(sectors)]
+    across_later = [is_later(1 - row, target) for target in targets]
+    along_later = [is_later(row, target) for target in targets]
+    across_tell = [(ordered & ~later) | is_root for later in across_later]
+    along_tell = [(ordered & ~later) | is_root for later in along_later]
+
+    has_up = slab < slabs - 1
+    has_down = slab > 0
+    over_root = (row == 0) & (me == 0) & (slab == 1)
+    wrap_up = has_up & (depth == DEPTHS - 1)
+    wrap_down = has_down & (depth == 0)
+    down_later = wrap_down | over_root
+    right_later = along_later[1]
+    left_later = along_later[sectors - 1]
+    neighbours = (
+        (has_up, wrap_up | is_root, None, {"span": slab + 1}, 0, 1),
+        (has_down & ~down_later, None, down_later, {"span": slab - 1}, 1, 0),
+        (~right_later, along_tell[1], right_later, {"sec": targets[1]}, 2, 3),
+        (~left_later, along_tell[sectors - 1], left_later, {"sec": targets[sectors - 1]}, 3, 2),
+    )
+
+    barrier = pltpu.get_barrier_semaphore()
+
+    def signal(sem, device):
+        pl.semaphore_signal(sem, inc=1, device_id=device, device_id_type=MESH)
+
+    def count(flags):
+        return sum(flag.astype(jnp.int32) for flag in flags)
+
+    for step, target in enumerate(targets):
+        pl.when(across_later[step] | ~across_tell[step])(
+            functools.partial(signal, barrier, {"row": 1 - row, "sec": target})
+        )
+        if step:
+            pl.when(along_later[step] | ~along_tell[step])(
+                functools.partial(signal, barrier, {"sec": target})
+            )
+    pl.when(has_up & ~wrap_up & ~is_root)(
+        functools.partial(signal, barrier, {"span": slab + 1})
+    )
+    pl.when(has_down)(functools.partial(signal, barrier, {"span": slab - 1}))
+
     loads = (
-        pltpu.make_async_copy(strip_src.at[:, 3], strip, load_sem.at[0]),
-        pltpu.make_async_copy(state_src, state, load_sem.at[1]),
-        pltpu.make_async_copy(visc_src, coeff, load_sem.at[2]),
+        pltpu.make_async_copy(state_src, state, load_sem.at[0]),
+        pltpu.make_async_copy(visc_src, coeff, load_sem.at[1]),
+        pltpu.make_async_copy(jac_src, jac, load_sem.at[2]),
+        pltpu.make_async_copy(freq_src, freq, load_sem.at[3]),
+        pltpu.make_async_copy(offs_src, offs, load_sem.at[4]),
     )
     for load in loads:
         load.start()
 
-    right = lax.rem(me + 1, sectors)
-    left = lax.rem(me + (sectors - 1), sectors)
-    has_up = slab < slabs - 1
-    has_down = slab > 0
-
-    barrier = pltpu.get_barrier_semaphore()
-
-    @pl.loop(0, sectors)
-    def _(step):
-        target = lax.rem(me + step, sectors)
-        pl.semaphore_signal(
-            barrier, inc=1, device_id={"row": 1 - row, "sec": target}, device_id_type=MESH
+    pl.semaphore_wait(
+        barrier,
+        2 * sectors
+        - 1
+        - count(across_later)
+        - count(along_later[1:])
+        + count((neighbours[0][0], neighbours[1][0])),
+    )
+    for _, told, _, device, _, there in neighbours:
+        if told is not None:
+            pl.when(told)(functools.partial(signal, ready_sem.at[there], device))
+
+    def spread(chosen):
+        for step, target in enumerate(targets):
+
+            @pl.when(is_holder(target) & chosen[step])
+            def _(target=target):
+                pltpu.make_async_remote_copy(
+                    src_ref=strip_src.at[pl.ds(share * rank(target), share), 3],
+                    dst_ref=gathered.at[me],
+                    send_sem=send_sem.at[0],
+                    recv_sem=recv_sem.at[0],
+                    device_id={"row": 1 - row, "sec": target},
+                    device_id_type=MESH,
+                ).start()
+
+    @pl.when(is_home)
+    def _():
+        for step, target in enumerate(targets):
+            pl.when(across_tell[step])(
+                functools.partial(signal, home_sem.at[0], {"row": 1 - row, "sec": target})
+            )
+
+    spread([~later for later in across_later])
+    for step in range(1, sectors):
+        pl.when(along_tell[step] & is_holder(targets[step]))(
+            functools.partial(signal, home_sem.at[1], {"sec": targets[step]})
         )
-
-        @pl.when(step > 0)
-        def _():
-            pl.semaphore_signal(
-                barrier, inc=1, device_id={"sec": target}, device_id_type=MESH
-            )
-
-    @pl.when(has_up)
-    def _():
-        pl.semaphore_signal(barrier, inc=1, device_id={"span": slab + 1}, device_id_type=MESH)
-
-    @pl.when(has_down)
-    def _():
-        pl.semaphore_signal(barrier, inc=1, device_id={"span": slab - 1}, device_id_type=MESH)
 
     for load in loads:
         load.wait()
 
     edge_up[...] = state[pl.ds(3, cells, stride=4), :]
     edge_down[...] = state[pl.ds(0, cells, stride=4), :]
+    to_right = pltpu.make_async_remote_copy(
+        src_ref=edges, dst_ref=edges_left, send_sem=send_sem.at[1], recv_sem=recv_sem.at[1],
+        device_id={"sec": targets[1]}, device_id_type=MESH,
+    )
+    to_left = pltpu.make_async_remote_copy(
+        src_ref=edges, dst_ref=edges_right, send_sem=send_sem.at[2], recv_sem=recv_sem.at[2],
+        device_id={"sec": targets[sectors - 1]}, device_id_type=MESH,
+    )
+    to_up = pltpu.make_async_remote_copy(
+        src_ref=edge_up, dst_ref=from_down, send_sem=send_sem.at[3], recv_sem=recv_sem.at[3],
+        device_id={"span": slab + 1}, device_id_type=MESH,
+    )
+    to_down = pltpu.make_async_remote_copy(
+        src_ref=edge_down, dst_ref=from_up, send_sem=send_sem.at[4], recv_sem=recv_sem.at[4],
+        device_id={"span": slab - 1}, device_id_type=MESH,
+    )
+    halos = tuple(zip((to_up, to_down, to_right, to_left), neighbours))
+    for halo, (earlier, _, _, _, _, _) in halos[:2]:
+        pl.when(earlier)(halo.start)
+
     lane = lax.broadcasted_iota(jnp.int32, (8, LANES), 1)
     sub = lax.broadcasted_iota(jnp.int32, (8, LANES), 0)
 
@@ -91,51 +202,8 @@
     edges[pl.ds(0, 8), :] = packed[0]
     edges[pl.ds(8, 8), :] = packed[1]
 
-    pl.semaphore_wait(
-        barrier, 2 * sectors - 1 + has_up.astype(jnp.int32) + has_down.astype(jnp.int32)
-    )
-
-    @pl.loop(0, sectors)
-    def _(step):
-        target = lax.rem(me + step, sectors)
-
-        @pl.when(target < holders)
-        def _():
-            pltpu.make_async_remote_copy(
-                src_ref=strip.at[pl.ds(share * target, share)],
-                dst_ref=gathered.at[me],
-                send_sem=send_sem.at[0],
-                recv_sem=recv_sem.at[0],
-                device_id={"row": 1 - row, "sec": target},
-                device_id_type=MESH,
-            ).start()
-
-    to_right = pltpu.make_async_remote_copy(
-        src_ref=edges, dst_ref=edges_left, send_sem=send_sem.at[1], recv_sem=recv_sem.at[1],
-        device_id={"sec": right}, device_id_type=MESH,
-    )
-    to_left = pltpu.make_async_remote_copy(
-        src_ref=edges, dst_ref=edges_right, send_sem=send_sem.at[2], recv_sem=recv_sem.at[2],
-        device_id={"sec": left}, device_id_type=MESH,
-    )
-    to_right.start()
-    to_left.start()
-    to_up = pltpu.make_async_remote_copy(
-        src_ref=edge_up, dst_ref=from_down, send_sem=send_sem.at[3], recv_sem=recv_sem.at[3],
-        device_id={"span": slab + 1}, device_id_type=MESH,
-    )
-    to_down = pltpu.make_async_remote_copy(
-        src_ref=edge_down, dst_ref=from_up, send_sem=send_sem.at[4], recv_sem=recv_sem.at[4],
-        device_id={"span": slab - 1}, device_id_type=MESH,
-    )
-
-    @pl.when(has_up)
-    def _():
-        to_up.start()
-
-    @pl.when(has_down)
-    def _():
-        to_down.start()
+    for halo, (earlier, _, _, _, _, _) in halos[2:]:
+        pl.when(earlier)(halo.start)
 
     weights = [
         freq[0] * jnp.float32(-0.05 * (-1.0) ** m / math.sin(math.pi * m / times))
@@ -157,39 +225,71 @@
                     acc = term if acc is None else acc + term
                 total[at[t], :] = acc
 
-    @pl.when(me < holders)
+    def send_later(index, now):
+        halo, (_, _, later, _, told, _) = halos[index]
+
+        @pl.when(later & now)
+        def _():
+            pl.semaphore_wait(ready_sem.at[told], 1)
+            halo.start()
+
+    across = count([later & is_holder(target) for later, target in zip(across_later, targets)])
+
+    @pl.when(across > 0)
+    def _():
+        pl.semaphore_wait(home_sem.at[0], across)
+        spread(across_later)
+
+    beside_root = (row == 0) & (slab == 0)
+    root_right = beside_root & (targets[1] == 0)
+    root_left = beside_root & (targets[sectors - 1] == 0)
+    send_later(2, ~root_right)
+    send_later(3, ~root_left)
+
+    @pl.when(is_home)
     def _():
         pltpu.make_async_copy(gathered, gathered, recv_sem.at[0]).wait()
+        along = count(along_later[1:])
+
+        @pl.when(along > 0)
+        def _():
+            pl.semaphore_wait(home_sem.at[1], along)
+
         thin = lax.broadcasted_iota(jnp.int32, (4, LANES), 1)
+        wholes, rests = [], []
         for part in range(share):
-            offset = offs[(share * me + part) // fields]
+            offset = offs[(share * mine + part) // fields]
             shift = jnp.where(row == 0, offset, annulus - offset)
-            whole = shift >> 7
-            rest = shift & (LANES - 1)
-            before = pltpu.roll(
-                gathered[lax.rem(2 * sectors - 1 - whole, sectors), part], rest, 1
-            )
-            for sector in range(sectors):
-                after = pltpu.roll(
-                    gathered[lax.rem(2 * sectors + sector - whole, sectors), part], rest, 1
-                )
-                turned[sector, part] = jnp.where(thin >= rest, after, before)
-                before = after
-        pltpu.make_async_copy(
-            turned.at[me], ghost.at[pl.ds(share * me, share)], recv_sem.at[5]
-        ).start()
-
-        @pl.loop(1, sectors)
-        def _(step):
+            wholes.append(shift >> 7)
+            rests.append(shift & (LANES - 1))
+
+        def source(sector, part):
+            at = lax.rem(sector + (2 * sectors - wholes[part]), sectors)
+            return pltpu.roll(gathered[at, part], rests[part], 1)
+
+        before = [source(me - 1, part) for part in range(share)]
+        there = ghost.at[pl.ds(share * mine, share)]
+        for step in range(sectors):
             target = lax.rem(me + step, sectors)
-            pltpu.make_async_remote_copy(
-                src_ref=turned.at[target],
-                dst_ref=ghost.at[pl.ds(share * me, share)],
-                send_sem=send_sem.at[5],
-                recv_sem=recv_sem.at[5],
-                device_id={"sec": target},
-                device_id_type=MESH,
-            ).start()
+            for part in range(share):
+                after = source(me + step, part)
+                turned[target, part] = jnp.where(thin >= rests[part], after, before[part])
+                before[part] = after
+            if step == 0:
+                pltpu.make_async_copy(turned.at[me], there, recv_sem.at[5]).start()
+            else:
+                pltpu.make_async_remote_copy(
+                    src_ref=turned.at[target],
+                    dst_ref=there,
+                    send_sem=send_sem.at[5],
+                    recv_sem=recv_sem.at[5],
+                    device_id={"sec": target},
+                    device_id_type=MESH,
+                ).start()
+
+    send_later(2, root_right)
+    send_later(3, root_left)
+    send_later(1, has_down)
 
     to_right.wait_recv()
     to_left.wait_recv()
@@ -281,9 +381,7 @@
         at = pl.ds(16 * n + 12, 4)
         total[at, :] = total[at, :] + 0.1 * ghost[n]
 
-    store = pltpu.make_async_copy(total, out, load_sem.at[0])
-    store.start()
-    pltpu.make_async_copy(strip, strip, send_sem.at[0]).wait()
+    pltpu.make_async_copy(ghost, ghost, send_sem.at[0]).wait()
     to_right.wait_send()
     to_left.wait_send()
 
@@ -295,12 +393,10 @@
     def _():
         to_down.wait_send()
 
-    @pl.when(me < holders)
+    @pl.when(is_home)
     def _():
         others = turned.at[pl.ds(0, sectors - 1)]
         pltpu.make_async_copy(others, others, send_sem.at[5]).wait()
-
-    store.wait()
 
 
 def solution(mesh):
@@ -309,32 +405,32 @@
     def on_device(state, viscosity, jacobian, frequency, offsets):
         _, times, fields, axial, span, lanes = state.shape
         planes = times * fields
-        share = next(
-            s for s in range(-(-planes // sectors), planes + 1) if planes % s == 0
-        )
+        share = planes // (sectors - len(AWAY))
         rows = planes * axial * span
         edge = pltpu.VMEM((planes * axial, lanes), jnp.float32)
         pairs = pltpu.VMEM((16, lanes), jnp.float32)
-        anywhere = pl.BlockSpec(memory_space=pl.ANY)
-        scalars = pl.BlockSpec(memory_space=pltpu.SMEM)
+        anywhere = pl.BlockSpec(memory_space=pltpu.HBM)
         out = pl.pallas_call(
-            functools.partial(kernel, sectors, slabs, times, fields, share),
-            out_shape=jax.ShapeDtypeStruct((rows, lanes), jnp.float32),
-            in_specs=[anywhere] * 3 + [scalars] * 3,
-            out_specs=anywhere,
+            functools.partial(kernel, sectors, slabs, times, fields, share, AWAY),
+            out_shape=pltpu.VMEM((rows, lanes), jnp.float32),
+            in_specs=[anywhere] * 6,
+            out_specs=pl.BlockSpec(memory_space=pltpu.VMEM),
             scratch_shapes=[
                 pltpu.VMEM((rows, lanes), jnp.float32),
-                pltpu.VMEM((planes, span, lanes), jnp.float32),
                 pltpu.VMEM((16, lanes), jnp.float32),
-                pltpu.VMEM((rows, lanes), jnp.float32),
+                pltpu.SMEM((fields, 1, fields), jnp.float32),
+                pltpu.SMEM((1,), jnp.float32),
+                pltpu.SMEM((times,), jnp.int32),
                 edge, edge, edge, edge,
                 pairs, pairs, pairs,
                 pltpu.VMEM((sectors, share, span, lanes), jnp.float32),
                 pltpu.VMEM((sectors, share, span, lanes), jnp.float32),
                 pltpu.VMEM((planes, span, lanes), jnp.float32),
-                pltpu.SemaphoreType.DMA((3,)),
+                pltpu.SemaphoreType.DMA((5,)),
                 pltpu.SemaphoreType.DMA((6,)),
                 pltpu.SemaphoreType.DMA((6,)),
+                pltpu.SemaphoreType.REGULAR((4,)),
+                pltpu.SemaphoreType.REGULAR((2,)),
             ],
             compiler_params=pltpu.CompilerParams(collective_id=0, has_side_effects=True),
         )(

time: 36.9 us -> 31.3 us (0.85)
  the two profiles are of different devices: /device:TPU:5 before, /device:TPU:207 now
where the time goes in v2:
time: 31.3 us; the launch traced here: 31.1 us
  Pallas kernels  29.7 us (95%)
  local copies, waits for them, and re-layouts  0.79 us (3%)
  between operations  0.66 us (2%)
    pallas_call x1, Pallas kernels, on_device(): pl.pallas_call(functools.partial(kernel, sectors, slabs, times, fields, s...  29.7 us
    unnamed x1, local copies, waits for them, and re-layouts  0.79 us

profile of v2, /device:TPU:207, one launch (start us, length us, event | category | flops | bytes accessed | tf_op | source)
XLA Modules:
  0.0 31.1 jit_solution(10160898236836685529)
XLA Ops:
  0.7 29.7 %shard_map.55 = f32[1008,128]{1,0:T(8,128)S(1)} custom-call(f32[63,4,4,128]{3,2,1,0:T(4,128)} %bitcast.6, f32[1008,128]{1,0:T(8,128)} %bitcast.7, f32[16,128]{1,0:T(8,128)} %bitcast.8, f32[7,1,7]{2,1,0:T(1,128)} %bitcast.9, f32[1]{0:T(128)S(6)} %copy.8.freq_src, s32[9]{0:T(128)} %offs_src.1), custom_call_target="tpu_custom_call" | custom-call | tf_op jit(solution)/shard_map/pallas_call | solution.py:413
  30.3 0.8 %copy.7 = f32[1,9,7,4,4,128]{5,4,3,2,1,0:T(4,128)} copy(f32[1,9,7,4,4,128]{5,4,3,2,1,0:T(4,128)S(1)} %bitcast.5) | data formatting | bytes 1032192

commit v3 on v2

--- a/solution.py
+++ b/solution.py
@@ -30,9 +30,6 @@
     cells = planes * 4
     annulus = sectors * LANES
 
-    right = lax.rem(me + 1, sectors)
-    left = lax.rem(me + (sectors - 1), sectors)
-
     def is_holder(sector):
         held = sector != away[0]
         for other in away[1:]:
@@ -62,28 +59,44 @@
     def root_at(at_row, sector):
         return (at_row == 0) & (sector == 0) & (slab == 0)
 
-    def is_later(at_row, sector):
-        return root_at(at_row, sector) | (ordered & ~is_root & (lateness(at_row, sector) > here))
-
     targets = [lax.rem(me + step, sectors) for step in range(sectors)]
-    across_later = [is_later(1 - row, target) for target in targets]
-    along_later = [is_later(row, target) for target in targets]
-    across_tell = [(ordered & ~later) | is_root for later in across_later]
-    along_tell = [(ordered & ~later) | is_root for later in along_later]
+    held = [is_holder(target) for target in targets]
+    far_first = sorted(range(sectors), key=lambda step: -min(step % 8, 8 - step % 8))
+
+    def choose(one, other):
+        return (ordered & one) | (~ordered & other)
+
+    across_later = [ordered & (lateness(1 - row, target) > here) for target in targets]
+    along_later = [lateness(row, target) > here for target in targets]
+    across_greet = [choose(later, is_home) for later in across_later]
+    across_wait = [choose(~later, at) for later, at in zip(across_later, held)]
+    along_greet, along_wait, along_tell, along_miss = [None], [None], [None], [None]
+    for step in range(1, sectors):
+        later, at = along_later[step], held[step]
+        greet, wait = is_home & ~at, ~is_home & at
+        if step in (1, sectors - 1):
+            greet, wait = greet | ~is_root, wait | ~root_at(row, targets[step])
+        along_greet.append(choose(later, greet))
+        along_wait.append(choose(~later, wait))
+        along_tell.append(choose(~later & at, ~is_home & at))
+        along_miss.append(choose(later, is_home & ~at))
 
     has_up = slab < slabs - 1
     has_down = slab > 0
-    over_root = (row == 0) & (me == 0) & (slab == 1)
-    wrap_up = has_up & (depth == DEPTHS - 1)
-    wrap_down = has_down & (depth == 0)
-    down_later = wrap_down | over_root
-    right_later = along_later[1]
-    left_later = along_later[sectors - 1]
+    up_later = has_up & (depth != DEPTHS - 1) & ~is_root
+    up_earlier = has_up & ~up_later
+    down_later = has_down & ((depth == 0) | ((row == 0) & (me == 0) & (slab == 1)))
+    down_earlier = has_down & ~down_later
+
+    def beside(step):
+        root, later = root_at(row, targets[step]), along_later[step]
+        return choose(~later, ~root), choose(~later, is_root), choose(later, root)
+
     neighbours = (
-        (has_up, wrap_up | is_root, None, {"span": slab + 1}, 0, 1),
-        (has_down & ~down_later, None, down_later, {"span": slab - 1}, 1, 0),
-        (~right_later, along_tell[1], right_later, {"sec": targets[1]}, 2, 3),
-        (~left_later, along_tell[sectors - 1], left_later, {"sec": targets[sectors - 1]}, 3, 2),
+        (up_earlier, up_earlier, up_later, {"span": slab + 1}, 0, 1),
+        (down_earlier, down_earlier, down_later, {"span": slab - 1}, 1, 0),
+        (*beside(1), {"sec": targets[1]}, 2, 3),
+        (*beside(sectors - 1), {"sec": targets[sectors - 1]}, 3, 2),
     )
 
     barrier = pltpu.get_barrier_semaphore()
@@ -94,18 +107,17 @@
     def count(flags):
         return sum(flag.astype(jnp.int32) for flag in flags)
 
-    for step, target in enumerate(targets):
-        pl.when(across_later[step] | ~across_tell[step])(
-            functools.partial(signal, barrier, {"row": 1 - row, "sec": target})
+    for step in far_first:
+        pl.when(across_greet[step])(
+            functools.partial(signal, barrier, {"row": 1 - row, "sec": targets[step]})
         )
+    for step in far_first:
         if step:
-            pl.when(along_later[step] | ~along_tell[step])(
-                functools.partial(signal, barrier, {"sec": target})
+            pl.when(along_greet[step])(
+                functools.partial(signal, barrier, {"sec": targets[step]})
             )
-    pl.when(has_up & ~wrap_up & ~is_root)(
-        functools.partial(signal, barrier, {"span": slab + 1})
-    )
-    pl.when(has_down)(functools.partial(signal, barrier, {"span": slab - 1}))
+    for _, _, later, device, _, _ in neighbours[:2]:
+        pl.when(later)(functools.partial(signal, barrier, device))
 
     loads = (
         pltpu.make_async_copy(state_src, state, load_sem.at[0]),
@@ -118,22 +130,16 @@
         load.start()
 
     pl.semaphore_wait(
-        barrier,
-        2 * sectors
-        - 1
-        - count(across_later)
-        - count(along_later[1:])
-        + count((neighbours[0][0], neighbours[1][0])),
+        barrier, count(across_wait + along_wait[1:] + [up_earlier, down_earlier])
     )
     for _, told, _, device, _, there in neighbours:
-        if told is not None:
-            pl.when(told)(functools.partial(signal, ready_sem.at[there], device))
+        pl.when(told)(functools.partial(signal, ready_sem.at[there], device))
 
     def spread(chosen):
-        for step, target in enumerate(targets):
-
-            @pl.when(is_holder(target) & chosen[step])
-            def _(target=target):
+        for step in far_first:
+
+            @pl.when(held[step] & chosen[step])
+            def _(target=targets[step]):
                 pltpu.make_async_remote_copy(
                     src_ref=strip_src.at[pl.ds(share * rank(target), share), 3],
                     dst_ref=gathered.at[me],
@@ -143,16 +149,18 @@
                     device_id_type=MESH,
                 ).start()
 
-    @pl.when(is_home)
-    def _():
-        for step, target in enumerate(targets):
-            pl.when(across_tell[step])(
-                functools.partial(signal, home_sem.at[0], {"row": 1 - row, "sec": target})
+    @pl.when(is_home & ordered)
+    def _():
+        for step in far_first:
+            pl.when(~across_later[step])(
+                functools.partial(
+                    signal, home_sem.at[0], {"row": 1 - row, "sec": targets[step]}
+                )
             )
 
     spread([~later for later in across_later])
     for step in range(1, sectors):
-        pl.when(along_tell[step] & is_holder(targets[step]))(
+        pl.when(along_tell[step])(
             functools.partial(signal, home_sem.at[1], {"sec": targets[step]})
         )
 
@@ -233,7 +241,7 @@
             pl.semaphore_wait(ready_sem.at[told], 1)
             halo.start()
 
-    across = count([later & is_holder(target) for later, target in zip(across_later, targets)])
+    across = count([later & at for later, at in zip(across_later, held)])
 
     @pl.when(across > 0)
     def _():
@@ -245,11 +253,13 @@
     root_left = beside_root & (targets[sectors - 1] == 0)
     send_later(2, ~root_right)
     send_later(3, ~root_left)
+    soon = (depth == DEPTHS - 2) | (depth == DEPTHS - 3)
+    send_later(0, soon)
 
     @pl.when(is_home)
     def _():
         pltpu.make_async_copy(gathered, gathered, recv_sem.at[0]).wait()
-        along = count(along_later[1:])
+        along = count(along_miss[1:])
 
         @pl.when(along > 0)
         def _():
@@ -289,6 +299,7 @@
 
     send_later(2, root_right)
     send_later(3, root_left)
+    send_later(0, ~soon)
     send_later(1, has_down)
 
     to_right.wait_recv()

time: 31.3 us -> 31 us (level)
  the two profiles are of different devices: /device:TPU:207 before, /device:TPU:30 now
where the time goes in v3:
time: 31 us; the launch traced here: 30.9 us
  Pallas kernels  29.4 us (95%)
  local copies, waits for them, and re-layouts  0.79 us (3%)
  between operations  0.66 us (2%)
    pallas_call x1, Pallas kernels, on_device(): pl.pallas_call(functools.partial(kernel, sectors, slabs, times, fields, s...  29.4 us
    unnamed x1, local copies, waits for them, and re-layouts  0.79 us

profile of v3, /device:TPU:30, one launch (start us, length us, event | category | flops | bytes accessed | tf_op | source)
XLA Modules:
  0.0 30.9 jit_solution(6718115294768334583)
XLA Ops:
  0.7 29.4 %shard_map.55 = f32[1008,128]{1,0:T(8,128)S(1)} custom-call(f32[63,4,4,128]{3,2,1,0:T(4,128)} %bitcast.6, f32[1008,128]{1,0:T(8,128)} %bitcast.7, f32[16,128]{1,0:T(8,128)} %bitcast.8, f32[7,1,7]{2,1,0:T(1,128)} %bitcast.9, f32[1]{0:T(128)S(6)} %copy.8.freq_src, s32[9]{0:T(128)} %offs_src.1), custom_call_target="tpu_custom_call" | custom-call | tf_op jit(solution)/shard_map/pallas_call | solution.py:424
  30.1 0.8 %copy.7 = f32[1,9,7,4,4,128]{5,4,3,2,1,0:T(4,128)} copy(f32[1,9,7,4,4,128]{5,4,3,2,1,0:T(4,128)S(1)} %bitcast.5) | data formatting | bytes 1032192

commit v4 on v3

--- a/solution.py
+++ b/solution.py
@@ -17,7 +17,7 @@
 def kernel(
     sectors, slabs, times, fields, share, away,
     strip_src, state_src, visc_src, jac_src, freq_src, offs_src, total,
-    state, coeff, jac, freq, offs,
+    state, strip, coeff, jac, freq, offs,
     edge_up, edge_down, from_up, from_down,
     edges, edges_left, edges_right,
     gathered, turned, ghost,
@@ -51,7 +51,7 @@
 
     def lateness(at_row, sector):
         along = sector & 7
-        late = 10 * jnp.minimum(along, 8 - along) + jnp.where(along > 3, 10, 0) + jnp.where(sector > 15, 14, 0)
+        late = 10 * jnp.minimum(along, 8 - along) + jnp.where(along > 3, 10, 0) + 60 * (sector >> 3)
         return late * (2 * sectors) + 2 * sector + at_row
 
     here = lateness(row, me)
@@ -119,6 +119,8 @@
     for _, _, later, device, _, _ in neighbours[:2]:
         pl.when(later)(functools.partial(signal, barrier, device))
 
+    planes_load = pltpu.make_async_copy(strip_src.at[:, 3], strip, load_sem.at[5])
+    planes_load.start()
     loads = (
         pltpu.make_async_copy(state_src, state, load_sem.at[0]),
         pltpu.make_async_copy(visc_src, coeff, load_sem.at[1]),
@@ -132,6 +134,7 @@
     pl.semaphore_wait(
         barrier, count(across_wait + along_wait[1:] + [up_earlier, down_earlier])
     )
+    planes_load.wait()
     for _, told, _, device, _, there in neighbours:
         pl.when(told)(functools.partial(signal, ready_sem.at[there], device))
 
@@ -141,7 +144,7 @@
             @pl.when(held[step] & chosen[step])
             def _(target=targets[step]):
                 pltpu.make_async_remote_copy(
-                    src_ref=strip_src.at[pl.ds(share * rank(target), share), 3],
+                    src_ref=strip.at[pl.ds(share * rank(target), share)],
                     dst_ref=gathered.at[me],
                     send_sem=send_sem.at[0],
                     recv_sem=recv_sem.at[0],
@@ -299,8 +302,8 @@
 
     send_later(2, root_right)
     send_later(3, root_left)
+    send_later(1, has_down)
     send_later(0, ~soon)
-    send_later(1, has_down)
 
     to_right.wait_recv()
     to_left.wait_recv()
@@ -428,6 +431,7 @@
             out_specs=pl.BlockSpec(memory_space=pltpu.VMEM),
             scratch_shapes=[
                 pltpu.VMEM((rows, lanes), jnp.float32),
+                pltpu.VMEM((planes, span, lanes), jnp.float32),
                 pltpu.VMEM((16, lanes), jnp.float32),
                 pltpu.SMEM((fields, 1, fields), jnp.float32),
                 pltpu.SMEM((1,), jnp.float32),
@@ -437,7 +441,7 @@
                 pltpu.VMEM((sectors, share, span, lanes), jnp.float32),
                 pltpu.VMEM((sectors, share, span, lanes), jnp.float32),
                 pltpu.VMEM((planes, span, lanes), jnp.float32),
-                pltpu.SemaphoreType.DMA((5,)),
+                pltpu.SemaphoreType.DMA((6,)),
                 pltpu.SemaphoreType.DMA((6,)),
                 pltpu.SemaphoreType.DMA((6,)),
                 pltpu.SemaphoreType.REGULAR((4,)),

time: 31 us -> 29.1 us (0.939)
  the two profiles are of different devices: /device:TPU:30 before, /device:TPU:249 now
where the time goes in v4:
time: 29.1 us; the launch traced here: 28.9 us
  Pallas kernels  27.5 us (95%)
  local copies, waits for them, and re-layouts  0.79 us (3%)
  between operations  0.66 us (2%)
    pallas_call x1, Pallas kernels, on_device(): pl.pallas_call(functools.partial(kernel, sectors, slabs, times, fields, s...  27.5 us
    unnamed x1, local copies, waits for them, and re-layouts  0.79 us

profile of v4, /device:TPU:249, one launch (start us, length us, event | category | flops | bytes accessed | tf_op | source)
XLA Modules:
  0.0 28.9 jit_solution(13539426556543731942)
XLA Ops:
  0.7 27.5 %shard_map.55 = f32[1008,128]{1,0:T(8,128)S(1)} custom-call(f32[63,4,4,128]{3,2,1,0:T(4,128)} %bitcast.6, f32[1008,128]{1,0:T(8,128)} %bitcast.7, f32[16,128]{1,0:T(8,128)} %bitcast.8, f32[7,1,7]{2,1,0:T(1,128)} %bitcast.9, f32[1]{0:T(128)S(6)} %copy.8.freq_src, s32[9]{0:T(128)} %offs_src.1), custom_call_target="tpu_custom_call" | custom-call | tf_op jit(solution)/shard_map/pallas_call | solution.py:427
  28.1 0.8 %copy.7 = f32[1,9,7,4,4,128]{5,4,3,2,1,0:T(4,128)} copy(f32[1,9,7,4,4,128]{5,4,3,2,1,0:T(4,128)S(1)} %bitcast.5) | data formatting | bytes 1032192

commit v5 on v4

--- a/solution.py
+++ b/solution.py
@@ -11,7 +11,7 @@
 MESH = pl.DeviceIdType.MESH
 LANES = 128
 DEPTHS = 4
-AWAY = (0, 12, 20)
+AWAY = (0, 20, 21)
 
 
 def kernel(
@@ -256,7 +256,7 @@
     root_left = beside_root & (targets[sectors - 1] == 0)
     send_later(2, ~root_right)
     send_later(3, ~root_left)
-    soon = (depth == DEPTHS - 2) | (depth == DEPTHS - 3)
+    soon = depth == DEPTHS - 2
     send_later(0, soon)
 
     @pl.when(is_home)
@@ -288,15 +288,15 @@
                 after = source(me + step, part)
                 turned[target, part] = jnp.where(thin >= rests[part], after, before[part])
                 before[part] = after
-            if step == 0:
-                pltpu.make_async_copy(turned.at[me], there, recv_sem.at[5]).start()
-            else:
+        pltpu.make_async_copy(turned.at[me], there, recv_sem.at[5]).start()
+        for step in far_first:
+            if step:
                 pltpu.make_async_remote_copy(
-                    src_ref=turned.at[target],
+                    src_ref=turned.at[targets[step]],
                     dst_ref=there,
                     send_sem=send_sem.at[5],
                     recv_sem=recv_sem.at[5],
-                    device_id={"sec": target},
+                    device_id={"sec": targets[step]},
                     device_id_type=MESH,
                 ).start()
 

time: 29.1 us -> 28.9 us (level)
  the two profiles are of different devices: /device:TPU:249 before, /device:TPU:85 now
where the time goes in v5:
time: 28.9 us; the launch traced here: 28.7 us
  Pallas kernels  27.3 us (94%)
  local copies, waits for them, and re-layouts  0.79 us (3%)
  between operations  0.66 us (2%)
    pallas_call x1, Pallas kernels, on_device(): pl.pallas_call(functools.partial(kernel, sectors, slabs, times, fields, s...  27.3 us
    unnamed x1, local copies, waits for them, and re-layouts  0.79 us

profile of v5, /device:TPU:85, one launch (start us, length us, event | category | flops | bytes accessed | tf_op | source)
XLA Modules:
  0.0 28.7 jit_solution(9163607982105339414)
XLA Ops:
  0.7 27.3 %shard_map.55 = f32[1008,128]{1,0:T(8,128)S(1)} custom-call(f32[63,4,4,128]{3,2,1,0:T(4,128)} %bitcast.6, f32[1008,128]{1,0:T(8,128)} %bitcast.7, f32[16,128]{1,0:T(8,128)} %bitcast.8, f32[7,1,7]{2,1,0:T(1,128)} %bitcast.9, f32[1]{0:T(128)S(6)} %copy.8.freq_src, s32[9]{0:T(128)} %offs_src.1), custom_call_target="tpu_custom_call" | custom-call | tf_op jit(solution)/shard_map/pallas_call | solution.py:427
  27.9 0.8 %copy.7 = f32[1,9,7,4,4,128]{5,4,3,2,1,0:T(4,128)} copy(f32[1,9,7,4,4,128]{5,4,3,2,1,0:T(4,128)S(1)} %bitcast.5) | data formatting | bytes 1032192

commit v6 on v4

--- a/solution.py
+++ b/solution.py
@@ -11,7 +11,7 @@
 MESH = pl.DeviceIdType.MESH
 LANES = 128
 DEPTHS = 4
-AWAY = (0, 12, 20)
+AWAY = (0, 20, 21)
 
 
 def kernel(

time: 29.1 us -> 28.9 us (level)
  the two profiles are of different devices: /device:TPU:249 before, /device:TPU:87 now
where the time goes in v6:
time: 28.9 us; the launch traced here: 28.7 us
  Pallas kernels  27.3 us (94%)
  local copies, waits for them, and re-layouts  0.79 us (3%)
  between operations  0.66 us (2%)
    pallas_call x1, Pallas kernels, on_device(): pl.pallas_call(functools.partial(kernel, sectors, slabs, times, fields, s...  27.3 us
    unnamed x1, local copies, waits for them, and re-layouts  0.79 us

profile of v6, /device:TPU:87, one launch (start us, length us, event | category | flops | bytes accessed | tf_op | source)
XLA Modules:
  0.0 28.7 jit_solution(17836945016668653605)
XLA Ops:
  0.7 27.3 %shard_map.55 = f32[1008,128]{1,0:T(8,128)S(1)} custom-call(f32[63,4,4,128]{3,2,1,0:T(4,128)} %bitcast.6, f32[1008,128]{1,0:T(8,128)} %bitcast.7, f32[16,128]{1,0:T(8,128)} %bitcast.8, f32[7,1,7]{2,1,0:T(1,128)} %bitcast.9, f32[1]{0:T(128)S(6)} %copy.8.freq_src, s32[9]{0:T(128)} %offs_src.1), custom_call_target="tpu_custom_call" | custom-call | tf_op jit(solution)/shard_map/pallas_call | solution.py:427
  28.0 0.8 %copy.7 = f32[1,9,7,4,4,128]{5,4,3,2,1,0:T(4,128)} copy(f32[1,9,7,4,4,128]{5,4,3,2,1,0:T(4,128)S(1)} %bitcast.5) | data formatting | bytes 1032192
